TPU v7x, 256 devices: a whole 4x4x8 slice. The times are simulated.
256 devices in a mesh: zonal: 64 (over y_lo, x, z), merid: 4 (over y_hi, core).
Axes of the slice: x: 4, y: 4 (y_hi: 2, y_lo: 2; y = y_hi * 2 + y_lo), z: 8, core: 2. Of those that a mesh axis runs over, the one named last changes fastest.
Arguments:
- field: bfloat16 [64, 4096, 256], P('merid', 'zonal'), may hold values from -6 to 6
- weight_one: bfloat16 [3, 3, 256, 256], replicated, may hold values from -0.125 to 0.125
- bias_one: float32 [256], replicated, may hold values from -3 to 3
- weight_two: bfloat16 [3, 3, 256, 256], replicated, may hold values from -0.125 to 0.125
- bias_two: float32 [256], replicated, may hold values from -3 to 3
- depth_levels: int32 [64, 4096], P('merid', 'zonal'), may hold values from 0 to 64
- fold_partner: int32 [4096], replicated, may hold values from 0 to 4095, as said below
- cotangent: bfloat16 [64, 4096, 256], P('merid', 'zonal'), may hold values from -6 to 6
Outputs:
- output: bfloat16 [64, 4096, 256], P('merid', 'zonal')
- input_grad: bfloat16 [64, 4096, 256], P('merid', 'zonal')
- grad_one: float32 [3, 3, 256, 256], replicated
- grad_two: float32 [3, 3, 256, 256], replicated
Inputs may be any that keep to these rules, and one draw needn't show every extreme that they name: fold_partner[i] = (4095 - i + s) mod 4096 with one pivot offset s, 0 to 4095, for the whole table.
All inputs are finite; a program needn't handle non-finite values.
Results may differ from a plain program's by a relative error of at most 0.003.
Values may be sent and summed in bfloat16 or wider, within the bound.
No kernel may reach another device: no remote copies, remote signals or barrier semaphores. Data moves between devices by JAX's collectives and lax.ppermute only.
A program may use at most 128 MiB of HBM per device.

v0:
```python
import math
import jax
import jax.numpy as jnp
from jax import lax
from jax.sharding import PartitionSpec as P

LEV = 64


def with_halo(cells, sides, width, closed):
    for axis, dim in sides:
        count = lax.axis_size(axis)
        ends = count if closed else count - 1
        head = lax.slice_in_dim(cells, 0, width, axis=dim)
        tail = lax.slice_in_dim(cells, cells.shape[dim] - width, cells.shape[dim], axis=dim)
        cells = jnp.concatenate(
            [
                lax.ppermute(tail, axis, [(i, (i + 1) % count) for i in range(ends)]),
                cells,
                lax.ppermute(head, axis, [((i + 1) % count, i) for i in range(ends)]),
            ],
            axis=dim,
        )
    return cells


def level_mask(depth_levels, channels):
    level_index = lax.broadcasted_iota(jnp.int32, (1, 1, channels), 2) % LEV
    return (level_index < depth_levels[:, :, None]).astype(jnp.float32)


def fold_forward(top_row, fold_partner):
    columns = top_row.shape[0]
    whole_row = lax.all_gather(top_row, "zonal", axis=0, tiled=True)
    partners = lax.dynamic_slice_in_dim(fold_partner, lax.axis_index("zonal") * columns, columns, 0)
    return jnp.take(whole_row, partners, axis=0)


def fold_backward(fold_grad, fold_partner):
    columns = fold_grad.shape[0]
    whole_row = lax.all_gather(fold_grad.astype(jnp.bfloat16), "zonal", axis=0, tiled=True).astype(
        fold_grad.dtype
    )
    partners = lax.dynamic_slice_in_dim(fold_partner, lax.axis_index("zonal") * columns, columns, 0)
    return jnp.take(whole_row, partners, axis=0)


def pad_field(values, fold_partner, is_top):
    with_rows = with_halo(values, (("merid", 0),), 1, False)
    fold_row = fold_forward(values[-1], fold_partner)
    upper_row = jnp.where(is_top, fold_row, with_rows[-1])
    with_rows = jnp.concatenate([with_rows[:-1], upper_row[None]], axis=0)
    return with_halo(with_rows, (("zonal", 1),), 1, True)


def unpad_grad(grad_pad, fold_partner, is_top):
    sides = jnp.concatenate([grad_pad[:, :1], grad_pad[:, -1:]], axis=1)
    returned = with_halo(sides.astype(jnp.bfloat16), (("zonal", 1),), 1, True).astype(sides.dtype)
    inner = grad_pad[:, 1:-1]
    inner = inner.at[:, 0].add(returned[:, 0]).at[:, -1].add(returned[:, 3])
    rims = jnp.concatenate([inner[:1], inner[-1:]], axis=0)
    back_rows = with_halo(rims.astype(jnp.bfloat16), (("merid", 0),), 1, False).astype(rims.dtype)
    folded = fold_backward(inner[-1], fold_partner)
    top_added = back_rows[3] + jnp.where(is_top, folded, jnp.zeros_like(folded))
    middle = inner[1:-1]
    return middle.at[0].add(back_rows[0]).at[-1].add(top_added)


def patches_of(padded, rows, columns):
    pieces = [
        padded[row_step : row_step + rows, col_step : col_step + columns]
        for row_step in range(3)
        for col_step in range(3)
    ]
    return jnp.concatenate(pieces, axis=2).reshape(rows * columns, -1)


def transpose_conv(delta, flat_weight, rows, columns):
    channels = delta.shape[1]
    parts = lax.dot_general(
        delta, flat_weight, (((1,), (1,)), ((), ())), preferred_element_type=jnp.float32
    )
    parts = parts.reshape(rows, columns, 9, channels)
    grad_pad = jnp.zeros((rows + 2, columns + 2, channels), jnp.float32)
    for row_step in range(3):
        for col_step in range(3):
            grad_pad = grad_pad.at[row_step : row_step + rows, col_step : col_step + columns].add(
                parts[:, :, 3 * row_step + col_step]
            )
    return grad_pad


def kernel_grad(patches, delta):
    channels = delta.shape[1]
    summed = lax.dot_general(
        patches, delta, (((0,), (0,)), ((), ())), preferred_element_type=jnp.float32
    )
    return summed.reshape(3, 3, channels, channels)


def shards(
    field, weight_one, bias_one, weight_two, bias_two, depth_levels, fold_partner, cotangent
):
    rows, columns, channels = field.shape
    is_top = lax.axis_index("merid") == lax.axis_size("merid") - 1
    mask = level_mask(depth_levels, channels)
    flat_one = weight_one.reshape(9 * channels, channels)
    flat_two = weight_two.reshape(9 * channels, channels)
    patches_one = patches_of(pad_field(field, fold_partner, is_top), rows, columns)
    pre_one = (
        jnp.dot(patches_one, flat_one, preferred_element_type=jnp.float32).reshape(
            rows, columns, channels
        )
        + bias_one
    )
    hidden = (jax.nn.gelu(pre_one) * mask).astype(jnp.bfloat16)
    patches_two = patches_of(pad_field(hidden, fold_partner, is_top), rows, columns)
    pre_two = jnp.dot(patches_two, flat_two, preferred_element_type=jnp.float32).reshape(
        rows, columns, channels
    )
    output = ((field.astype(jnp.float32) + pre_two + bias_two) * mask).astype(jnp.bfloat16)
    masked_grad = cotangent.astype(jnp.float32) * mask
    delta_two = masked_grad.astype(jnp.bfloat16).reshape(rows * columns, channels)
    grad_two = kernel_grad(patches_two, delta_two)
    hidden_grad = unpad_grad(
        transpose_conv(delta_two, flat_two, rows, columns), fold_partner, is_top
    )
    _, gelu_back = jax.vjp(jax.nn.gelu, pre_one)
    delta_one = (
        gelu_back(hidden_grad * mask)[0].astype(jnp.bfloat16).reshape(rows * columns, channels)
    )
    grad_one = kernel_grad(patches_one, delta_one)
    field_grad = unpad_grad(
        transpose_conv(delta_one, flat_one, rows, columns), fold_partner, is_top
    )
    input_grad = (masked_grad + field_grad).astype(jnp.bfloat16)
    grad_one, grad_two = lax.psum((grad_one, grad_two), ("zonal", "merid"))
    scale = 1.0 / math.sqrt(rows * columns * lax.axis_size("zonal") * lax.axis_size("merid"))
    return (output, input_grad, grad_one * scale, grad_two * scale)


def solution(mesh):
    placed = (
        P("merid", "zonal", None),
        P(),
        P(),
        P(),
        P(),
        P("merid", "zonal"),
        P(),
        P("merid", "zonal", None),
    )
    return jax.shard_map(
        shards,
        mesh=mesh,
        in_specs=placed,
        out_specs=(P("merid", "zonal", None), P("merid", "zonal", None), P(), P()),
        check_vma=False,
    )
```

profile of v0, /device:TPU:97, one launch (start us, length us, event | category | flops | bytes accessed | tf_op | source)
XLA Modules:
  0.0 1509.0 jit_solution(12286972379343277605)
XLA Ops:
  10.1 2.9 fusion.35
  14.0 2.7 copy-done.2
  16.6 2.4 fusion.27
  19.0 6.4 scatter-add.89
  26.8 4.3 add_select_fusion.1
  31.1 6.4 scatter-add.90
  39.0 2.4 fusion.24
  41.3 5.1 scatter-add.94
  46.5 2.4 fusion.23
  48.8 5.1 scatter-add.95
  55.4 2.4 fusion.20
  57.8 5.1 scatter-add.99
  62.9 2.4 fusion.19
  65.3 5.1 scatter-add.100
  70.5 2.9 collective-permute-start.8
  74.6 2.7 collective-permute-done.9
  83.2 6.8 collective-permute-start
  94.1 5.1 collective-permute-start.10
  101.2 157.8 %all-gather.9.cloned.1.call-done = bf16[1,4096,256]{2,1,0:T(8,128)(2,1)} async-done(((bf16[1,64,256]{2,1,0:T(8,128)(2,1)}), bf16[1,4096,256]{2,1,0:T(8,128)(2,1)}) %all-gather.9.cloned.1.call-update) | async-done | bytes 2097168 | tf_op jit(solution)/shard_map/all_gather | solution.py:34
  259.0 2.5 gather_fusion
  262.9 3.3 collective-permute-start.3
  276.2 282.4 %all-gather.13.cloned.1.call-done = bf16[1,4096,256]{2,1,0:T(8,128)(2,1)} async-done(((bf16[1,64,256]{2,1,0:T(8,128)(2,1)}), bf16[1,4096,256]{2,1,0:T(8,128)(2,1)}) %all-gather.13.cloned.1.call-update) | async-done | bytes 2097168 | tf_op jit(solution)/shard_map/all_gather | solution.py:41
  558.5 3.9 bitcast_convert_fusion.1
  562.4 2.8 gather_fusion.2
  565.4 5.2 fusion.8
  571.3 2.5 fusion.33
  574.0 3.4 copy-done.3
  579.7 6.4 scatter-add.110
  586.1 3.3 add_select_fusion
  589.4 3.3 scatter-add.111
  610.6 3.1 collective-permute-start.13
  619.2 50.8 %collective-permute-start.5 = (bf16[1,64,256]{2,1,0:T(8,128)(2,1)}, bf16[1,64,256]{2,1,0:T(8,128)(2,1)S(1)}, u32[]{:S(2)}, u32[]{:S(2)}) collective-permute-start(bf16[1,64,256]{2,1,0:T(8,128)(2,1)} %get-tuple-element.341), channel_id=1, source_target_pairs={{1,0},{2,1},{3,2},{5,4},{6,5},{7,6},{9,8},{10,9},{11,10},{13,12},{... | collective-permute-start | bytes 98312 | tf_op jit(solution)/shard_map/ppermute | solution.py:20
  670.0 4.3 collective-permute-start.4
  674.3 6.8 copy.30
  681.1 187.6 %all-gather.11.cloned.1.call-done = bf16[1,4096,256]{2,1,0:T(8,128)(2,1)} async-done(((bf16[1,64,256]{2,1,0:T(8,128)(2,1)}), bf16[1,4096,256]{2,1,0:T(8,128)(2,1)}) %all-gather.11.cloned.1.call-update) | async-done | bytes 2097168 | tf_op jit(solution)/shard_map/all_gather | solution.py:34
  868.7 2.6 gather_fusion.1
  873.5 2.5 collective-permute-start.7
  876.0 5.1 fusion.55
  884.6 6.8 copy.31
  891.4 5.1 fusion.56
  897.3 52.6 %collective-permute-start.14 = (bf16[1,64,256]{2,1,0:T(8,128)(2,1)S(1)}, bf16[1,64,256]{2,1,0:T(8,128)(2,1)S(1)}, u32[]{:S(2)}, u32[]{:S(2)}) collective-permute-start(bf16[1,64,256]{2,1,0:T(8,128)(2,1)S(1)} %copy-done.14), channel_id=1, source_target_pairs={{0,1},{1,2},{2,3},{4,5},{5,6},{6,7},{8,9},{9,10},{10,11},{12,13},{... | collective-permute-start | bytes 98312 | tf_op jit(solution)/shard_map/ppermute | solution.py:18
  951.9 4.7 collective-permute-done.15
  956.7 211.5 %all-gather.15.cloned.1.call-done = bf16[1,4096,256]{2,1,0:T(8,128)(2,1)} async-done(((bf16[1,64,256]{2,1,0:T(8,128)(2,1)}), bf16[1,4096,256]{2,1,0:T(8,128)(2,1)}) %all-gather.15.cloned.1.call-update) | async-done | bytes 2097168 | tf_op jit(solution)/shard_map/all_gather | solution.py:41
  1168.2 3.9 bitcast_convert_fusion
  1172.0 3.0 gather_fusion.3
  1176.3 4.5 fusion.1
  1180.8 316.5 %all-reduce.5.cloned.1.call-done = (f32[3,3,256,256]{3,2,1,0:T(8,128)}, f32[3,3,256,256]{3,2,1,0:T(8,128)}) async-done(((f32[3,3,256,256]{3,2,1,0:T(8,128)}, f32[3,3,256,256]{3,2,1,0:T(8,128)}), (f32[3,3,256,256]{3,2,1,0:T(8,128)}, f32[3,3,256,256]{3,2,1,0:T(8,128)})) %all-reduce.5.cloned.1.call-update) | async-done | bytes 4718608 | tf_op jit(solution)/shard_map/psum | solution.py:137
  1497.3 5.1 broadcast_multiply_fusion
  (164 shorter events, 68.6 us)
Async XLA Ops:
  7.2 558.2 %copy-start = (bf16[3,3,256,256]{3,2,1,0:T(8,128)(2,1)S(1)}, bf16[3,3,256,256]{3,2,1,0:T(8,128)(2,1)}, u32[]{:S(2)}) copy-start(bf16[3,3,256,256]{3,2,1,0:T(8,128)(2,1)} %param.65) | copy-start | bytes 3538948
  7.2 251.8 %all-gather.9.cloned.1.call-start = ((), (), s32[]{:S(2)}) async-start(), calls=%async_computation | async-start | bytes 2129920 | tf_op jit(solution)/shard_map/all_gather | solution.py:34
  8.7 549.8 %all-gather.13.cloned.1.call-start = ((), (), s32[]{:S(2)}) async-start(), calls=%async_computation.2 | async-start | bytes 2129920 | tf_op jit(solution)/shard_map/all_gather | solution.py:41
  8.8 556.6 %copy-start.25 = (s32[256]{0:T(256)}, s32[256]{0:T(256)S(1)}, u32[]{:S(2)}) copy-start(s32[256]{0:T(256)S(1)} %and_select_fusion) | copy-start | bytes 3076
  10.1 2.9 copy-start.8
  13.0 3.7 copy-start.2
  16.6 9.5 copy-start.27
  70.4 12.8 copy-start.17
  70.5 4.1 collective-permute-start.8
  73.4 188.2 %copy-start.4 = (bf16[16,64,256]{2,1,0:T(8,128)(2,1)S(1)}, bf16[16,64,256]{2,1,0:T(8,128)(2,1)}, u32[]{:S(2)}) copy-start(bf16[16,64,256]{2,1,0:T(8,128)(2,1)} %param.64) | copy-start | bytes 1572868
  73.4 3.8 collective-permute-start.9
  83.2 183.1 %copy-start.13 = (bf16[1,64,256]{2,1,0:T(8,128)(2,1)S(1)}, bf16[1,64,256]{2,1,0:T(8,128)(2,1)}, u32[]{:S(2)}) copy-start(bf16[1,64,256]{2,1,0:T(8,128)(2,1)} %get-tuple-element.324) | copy-start | bytes 98308
  83.2 785.5 %all-gather.11.cloned.1.call-start = ((), (), s32[]{:S(2)}) async-start(), calls=%async_computation.1 | async-start | bytes 2129920 | tf_op jit(solution)/shard_map/all_gather | solution.py:34
  83.2 178.4 %collective-permute-start = (bf16[1,64,256]{2,1,0:T(8,128)(2,1)S(1)}, bf16[1,64,256]{2,1,0:T(8,128)(2,1)S(1)}, u32[]{:S(2)}, u32[]{:S(2)}) collective-permute-start(bf16[1,64,256]{2,1,0:T(8,128)(2,1)S(1)} %copy-done.17), channel_id=1, source_target_pairs={{0,1},{1,2},{2,3},{4,5},{5,6},{6,7},{8,9},{9,10},{10,11},{12,13},{... | collective-permute-start | bytes 98312 | tf_op jit(solution)/shard_map/ppermute | solution.py:18
  90.1 171.5 %collective-permute-start.1 = (bf16[1,64,256]{2,1,0:T(8,128)(2,1)S(1)}, bf16[1,64,256]{2,1,0:T(8,128)(2,1)S(1)}, u32[]{:S(2)}, u32[]{:S(2)}) collective-permute-start(bf16[1,64,256]{2,1,0:T(8,128)(2,1)S(1)} %get-tuple-element.343), channel_id=1, source_target_pairs={{1,0},{2,1},{3,2},{5,4},{6,5},{7,6},{9,8},{10,9},{11,10},{13,12},{... | collective-permute-start | bytes 98312 | tf_op jit(solution)/shard_map/ppermute | solution.py:20
  92.8 472.5 %copy-start.22 = (pred[64]{0:T(512)(128)(4,1)}, pred[64]{0:T(512)(128)(4,1)S(1)}, u32[]{:S(2)}) copy-start(pred[64]{0:T(512)(128)(4,1)S(1)} %get-tuple-element.320) | copy-start | bytes 196
  92.8 469.7 %copy-start.24 = (s32[1024]{0:T(1024)}, s32[1024]{0:T(1024)S(1)}, u32[]{:S(2)}) copy-start(s32[1024]{0:T(1024)S(1)} %pad_clamp_fusion) | copy-start | bytes 12292
  94.1 172.1 %collective-permute-start.10 = (bf16[1,64,256]{2,1,0:T(8,128)(2,1)}, bf16[1,64,256]{2,1,0:T(8,128)(2,1)S(1)}, u32[]{:S(2)}, u32[]{:S(2)}) collective-permute-start(bf16[1,64,256]{2,1,0:T(8,128)(2,1)} %get-tuple-element.324), channel_id=1, source_target_pairs={{0,1},{1,2},{2,3},{4,5},{5,6},{6,7},{8,9},{9,10},{10,11},{12,13},{... | collective-permute-start | bytes 98312 | tf_op jit(solution)/shard_map/ppermute | solution.py:18
  99.3 167.0 %collective-permute-start.11 = (bf16[1,64,256]{2,1,0:T(8,128)(2,1)S(1)}, bf16[1,64,256]{2,1,0:T(8,128)(2,1)S(1)}, u32[]{:S(2)}, u32[]{:S(2)}) collective-permute-start(bf16[1,64,256]{2,1,0:T(8,128)(2,1)S(1)} %get-tuple-element.325), channel_id=1, source_target_pairs={{1,0},{2,1},{3,2},{5,4},{6,5},{7,6},{9,8},{10,9},{11,10},{13,12},{... | collective-permute-start | bytes 98312 | tf_op jit(solution)/shard_map/ppermute | solution.py:20
  261.7 5.7 collective-permute-start.2
  262.9 4.4 collective-permute-start.3
  276.2 289.3 %copy-start.20 = (s32[16,64]{1,0:T(8,128)S(1)}, s32[16,64]{1,0:T(8,128)}, u32[]{:S(2)}) copy-start(s32[16,64]{1,0:T(8,128)} %param.69) | copy-start | bytes 12292
  276.2 289.3 %copy-start.28 = (f32[256]{0:T(256)S(1)}, f32[256]{0:T(256)}, u32[]{:S(2)}) copy-start(f32[256]{0:T(256)} %param.66) | copy-start | bytes 3076
  571.2 596.9 %all-gather.15.cloned.1.call-start = ((), (), s32[]{:S(2)}) async-start(), calls=%async_computation.3 | async-start | bytes 2129920 | tf_op jit(solution)/shard_map/all_gather | solution.py:41
  573.8 3.6 copy-start.3
  609.3 5.5 copy-start.15
  609.3 5.5 copy-start.16
  609.3 5.5 collective-permute-start.12
  610.6 4.2 collective-permute-start.13
  618.4 62.7 %copy-start.6 = (f32[18,64,256]{2,1,0:T(8,128)}, f32[18,64,256]{2,1,0:T(8,128)S(1)}, u32[]{:S(2)}) copy-start(f32[18,64,256]{2,1,0:T(8,128)S(1)} %scatter-add.125) | copy-start | bytes 3538948
  619.1 878.2 %all-reduce.5.cloned.1.call-start = ((), (), s32[]{:S(2)}) async-start(), calls=%async_computation.4 | async-start | bytes 9437184 | tf_op jit(solution)/shard_map/psum | solution.py:137
  619.2 252.2 %collective-permute-start.5 = (bf16[1,64,256]{2,1,0:T(8,128)(2,1)}, bf16[1,64,256]{2,1,0:T(8,128)(2,1)S(1)}, u32[]{:S(2)}, u32[]{:S(2)}) collective-permute-start(bf16[1,64,256]{2,1,0:T(8,128)(2,1)} %get-tuple-element.341), channel_id=1, source_target_pairs={{1,0},{2,1},{3,2},{5,4},{6,5},{7,6},{9,8},{10,9},{11,10},{13,12},{... | collective-permute-start | bytes 98312 | tf_op jit(solution)/shard_map/ppermute | solution.py:20
  670.0 201.4 %collective-permute-start.4 = (bf16[1,64,256]{2,1,0:T(8,128)(2,1)}, bf16[1,64,256]{2,1,0:T(8,128)(2,1)S(1)}, u32[]{:S(2)}, u32[]{:S(2)}) collective-permute-start(bf16[1,64,256]{2,1,0:T(8,128)(2,1)} %get-tuple-element.340), channel_id=1, source_target_pairs={{0,1},{1,2},{2,3},{4,5},{5,6},{6,7},{8,9},{9,10},{10,11},{12,13},{... | collective-permute-start | bytes 98312 | tf_op jit(solution)/shard_map/ppermute | solution.py:18
  674.3 197.0 %copy-start.23 = (pred[64]{0:T(512)(128)(4,1)S(1)}, pred[64]{0:T(512)(128)(4,1)}, u32[]{:S(2)}) copy-start(pred[64]{0:T(512)(128)(4,1)} %copy-done.22) | copy-start | bytes 196
  674.3 201.7 %copy-start.12 = (bf16[16,64,256]{2,1,0:T(8,128)(2,1)S(1)}, bf16[16,64,256]{2,1,0:T(8,128)(2,1)}, u32[]{:S(2)}) copy-start(bf16[16,64,256]{2,1,0:T(8,128)(2,1)} %get-tuple-element.326) | copy-start | bytes 1572868
  871.5 9.7 collective-permute-start.6
  873.5 7.7 collective-permute-start.7
  882.4 2.2 copy-start.5
  884.6 6.8 copy-start.9
  896.5 55.3 %copy-start.7 = (f32[18,64,256]{2,1,0:T(8,128)S(1)}, f32[18,64,256]{2,1,0:T(8,128)}, u32[]{:S(2)}) copy-start(f32[18,64,256]{2,1,0:T(8,128)} %copy-done.6) | copy-start | bytes 3538948
  897.3 54.6 %collective-permute-start.14 = (bf16[1,64,256]{2,1,0:T(8,128)(2,1)S(1)}, bf16[1,64,256]{2,1,0:T(8,128)(2,1)S(1)}, u32[]{:S(2)}, u32[]{:S(2)}) collective-permute-start(bf16[1,64,256]{2,1,0:T(8,128)(2,1)S(1)} %copy-done.14), channel_id=1, source_target_pairs={{0,1},{1,2},{2,3},{4,5},{5,6},{6,7},{8,9},{9,10},{10,11},{12,13},{... | collective-permute-start | bytes 98312 | tf_op jit(solution)/shard_map/ppermute | solution.py:18
  949.9 6.7 collective-permute-start.15
  956.6 218.5 %copy-start.10 = (bf16[16,64,256]{2,1,0:T(8,128)(2,1)S(1)}, bf16[16,64,256]{2,1,0:T(8,128)(2,1)}, u32[]{:S(2)}) copy-start(bf16[16,64,256]{2,1,0:T(8,128)(2,1)} %param.71) | copy-start | bytes 1572868
  956.6 218.5 %copy-start.21 = (s32[16,64]{1,0:T(8,128)S(1)}, s32[16,64]{1,0:T(8,128)}, u32[]{:S(2)}) copy-start(s32[16,64]{1,0:T(8,128)} %param.69) | copy-start | bytes 12292
  956.6 218.5 %copy-start.26 = (s32[256]{0:T(256)S(1)}, s32[256]{0:T(256)}, u32[]{:S(2)}) copy-start(s32[256]{0:T(256)} %copy-done.25) | copy-start | bytes 3076
  1172.0 4.2 copy-start.29
  1175.0 1.3 copy-start.11
  1497.3 5.1 copy-start.1
  (3 other events, 2.0 us)
Sparse Core Ops, SparseCore 0:
  10.4 248.6 all-gather.8
  261.4 297.1 all-gather.12
  571.4 297.2 all-gather.10
  870.3 297.7 all-gather.14
  1174.2 323.0 all-reduce.4
where the time goes:
time: 1510 us
  waiting for transfers between devices  1160 us (77%)
  starting transfers between devices  142 us (9%)
  local copies, waits for them, and re-layouts  106 us (7%)
  other arithmetic  56.4 us (4%)
  matrix products  25.3 us (2%)
    all_gather x2, waiting for transfers between devices, fold_backward(): lax.all_gather(fold_grad.astype(jnp.bfloat16), 'zonal', axis=0, tiled=True)  494 us
    all_gather x2, waiting for transfers between devices, fold_forward(): whole_row = lax.all_gather(top_row, 'zonal', axis=0, tiled=True)  345 us
    psum x1, waiting for transfers between devices, shards(): grad_one, grad_two = lax.psum((grad_one, grad_two), ('zonal', 'merid'))  317 us
    ppermute x8, starting transfers between devices, with_halo(): lax.ppermute(tail, axis, [(i, (i + 1) % count) for i in range(ends)])  76.3 us
    ppermute x8, starting transfers between devices, with_halo(): lax.ppermute(head, axis, [((i + 1) % count, i) for i in range(ends)])  65.5 us
    scatter-add x14, local copies, waits for them, and re-layouts, transpose_conv(): grad_pad.at[row_step:row_step + rows, col_step:col_step + columns]  51.2 us
  transfers between devices with their start and end apart: 21, of which 9 were waited for; matrix products, arithmetic and copies ran while one was open for 10% of the time, Pallas kernels for 0%

commit v1 on v0

--- a/solution.py
+++ b/solution.py
@@ -31,7 +31,9 @@
 
 def fold_forward(top_row, fold_partner):
     columns = top_row.shape[0]
-    whole_row = lax.all_gather(top_row, "zonal", axis=0, tiled=True)
+    whole_row = jnp.concatenate(
+        lax.all_to_all(jnp.stack([top_row] * lax.axis_size("zonal")), "zonal", 0, 0), axis=0
+    )
     partners = lax.dynamic_slice_in_dim(fold_partner, lax.axis_index("zonal") * columns, columns, 0)
     return jnp.take(whole_row, partners, axis=0)
 

time: 1510 us -> 1060 us (0.70)
  waiting for transfers between devices: 1160 us -> 739 us
  starting transfers between devices: 142 us -> 116 us
    all_gather x2 -> x0, waiting for transfers between devices: 345 us -> none  [fold_forward(): whole_row = lax.all_gather(top_row, 'zonal', axis=0, tiled=True)]
    all_gather x2, waiting for transfers between devices: 494 us -> 414 us  [fold_backward(): lax.all_gather(fold_grad.astype(jnp.bfloat16), 'zonal', axis=0, tiled=True)]
    ppermute x8, starting transfers between devices: 76.3 us -> 32.1 us  [with_halo(): lax.ppermute(tail, axis, [(i, (i + 1) % count) for i in range(ends)])]
    all_to_all x0 -> x2, starting transfers between devices: none -> 24.1 us  [fold_forward(): lax.all_to_all(jnp.stack([top_row] * lax.axis_size('zonal')), 'zonal', 0, 0)]
  transfers between devices with their start and end apart: 21 -> 21, of which waited for: 9 -> 8; matrix products, arithmetic and copies ran while one was open for 10% -> 15% of each run, Pallas kernels for 0% -> 0%
where the time goes in v1:
time: 1060 us
  waiting for transfers between devices  739 us (70%)
  starting transfers between devices  116 us (11%)
  local copies, waits for them, and re-layouts  107 us (10%)
  other arithmetic  55.5 us (5%)
  matrix products  22.8 us (2%)
  between operations  14.6 us (1%)
    all_gather x2, waiting for transfers between devices, fold_backward(): lax.all_gather(fold_grad.astype(jnp.bfloat16), 'zonal', axis=0, tiled=True)  414 us
    psum x1, waiting for transfers between devices, shards(): grad_one, grad_two = lax.psum((grad_one, grad_two), ('zonal', 'merid'))  318 us
    ppermute x8, starting transfers between devices, with_halo(): lax.ppermute(head, axis, [((i + 1) % count, i) for i in range(ends)])  60.2 us
    scatter-add x14, local copies, waits for them, and re-layouts, transpose_conv(): grad_pad.at[row_step:row_step + rows, col_step:col_step + columns]  51.1 us
    ppermute x8, starting transfers between devices, with_halo(): lax.ppermute(tail, axis, [(i, (i + 1) % count) for i in range(ends)])  32.1 us
    all_to_all x2, starting transfers between devices, fold_forward(): lax.all_to_all(jnp.stack([top_row] * lax.axis_size('zonal')), 'zonal', 0, 0)  24.1 us
  transfers between devices with their start and end apart: 21, of which 8 were waited for; matrix products, arithmetic and copies ran while one was open for 15% of the time, Pallas kernels for 0%

profile of v1, /device:TPU:97, one launch (start us, length us, event | category | flops | bytes accessed | tf_op | source)
XLA Modules:
  0.0 1055.1 jit_solution(16497872787932612438)
XLA Ops:
  9.6 11.5 %all-to-all-start = ((bf16[64,64,256]{2,1,0:T(8,128)(2,1)}), bf16[64,64,256]{2,1,0:T(8,128)(2,1)}, u32[]{:S(2)}, u32[]{:S(2)}) async-start(bf16[64,64,256]{2,1,0:T(8,128)(2,1)} %stack.6), calls=%async_computation | async-start | bytes 4194304 | tf_op jit(solution)/shard_map/all_to_all | solution.py:35
  25.3 2.5 copy-done.3
  27.7 2.4 fusion.27
  30.1 6.4 scatter-add.89
  36.5 4.2 add_select_fusion.1
  40.7 6.4 scatter-add.90
  48.5 2.4 fusion.24
  50.9 5.1 scatter-add.94
  56.0 2.4 fusion.23
  58.4 5.1 scatter-add.95
  64.9 2.4 fusion.20
  67.3 5.1 scatter-add.99
  72.4 2.4 fusion.19
  74.8 5.1 scatter-add.100
  80.1 2.5 collective-permute-start.8
  83.7 2.7 collective-permute-done.9
  92.3 7.1 collective-permute-start
  102.1 5.1 collective-permute-start.10
  110.5 2.5 gather_fusion
  113.3 2.7 collective-permute-start.2
  125.9 215.2 %all-gather.5.cloned.1.call-done = bf16[1,4096,256]{2,1,0:T(8,128)(2,1)} async-done(((bf16[1,64,256]{2,1,0:T(8,128)(2,1)}), bf16[1,4096,256]{2,1,0:T(8,128)(2,1)}) %all-gather.5.cloned.1.call-update) | async-done | bytes 2097168 | tf_op jit(solution)/shard_map/all_gather | solution.py:43
  341.1 3.9 bitcast_convert_fusion.1
  345.0 2.8 gather_fusion.2
  348.0 5.2 fusion.8
  355.4 12.7 %all-to-all-start.1 = ((bf16[64,64,256]{2,1,0:T(8,128)(2,1)}), bf16[64,64,256]{2,1,0:T(8,128)(2,1)}, u32[]{:S(2)}, u32[]{:S(2)}) async-start(bf16[64,64,256]{2,1,0:T(8,128)(2,1)} %stack.7), calls=%async_computation.1 | async-start | bytes 4194304 | tf_op jit(solution)/shard_map/all_to_all | solution.py:35
  369.8 3.4 copy-done.2
  373.1 2.4 fusion.18
  375.5 6.4 scatter-add.110
  381.9 3.2 add_select_fusion
  385.1 3.2 scatter-add.111
  405.0 2.5 collective-permute-start.12
  408.3 2.9 collective-permute-done.13
  415.1 53.9 %collective-permute-start.5 = (bf16[1,64,256]{2,1,0:T(8,128)(2,1)}, bf16[1,64,256]{2,1,0:T(8,128)(2,1)S(1)}, u32[]{:S(2)}, u32[]{:S(2)}) collective-permute-start(bf16[1,64,256]{2,1,0:T(8,128)(2,1)} %get-tuple-element.342), channel_id=1, source_target_pairs={{1,0},{2,1},{3,2},{5,4},{6,5},{7,6},{9,8},{10,9},{11,10},{13,12},{... | collective-permute-start | bytes 98312 | tf_op jit(solution)/shard_map/ppermute | solution.py:20
  469.1 6.8 copy.30
  475.8 4.4 collective-permute-start.4
  480.3 2.6 gather_fusion.1
  483.4 2.7 collective-permute-start.6
  486.0 5.1 fusion.55
  492.5 2.2 copy-done.5
  494.6 6.8 copy.31
  501.4 5.1 fusion.56
  508.6 5.1 collective-permute-start.14
  514.8 198.4 %all-gather.7.cloned.1.call-done = bf16[1,4096,256]{2,1,0:T(8,128)(2,1)} async-done(((bf16[1,64,256]{2,1,0:T(8,128)(2,1)}), bf16[1,4096,256]{2,1,0:T(8,128)(2,1)}) %all-gather.7.cloned.1.call-update) | async-done | bytes 2097168 | tf_op jit(solution)/shard_map/all_gather | solution.py:43
  713.2 3.9 bitcast_convert_fusion
  717.0 3.0 gather_fusion.3
  721.3 4.5 fusion.1
  725.8 317.7 %all-reduce.5.cloned.1.call-done = (f32[3,3,256,256]{3,2,1,0:T(8,128)}, f32[3,3,256,256]{3,2,1,0:T(8,128)}) async-done(((f32[3,3,256,256]{3,2,1,0:T(8,128)}, f32[3,3,256,256]{3,2,1,0:T(8,128)}), (f32[3,3,256,256]{3,2,1,0:T(8,128)}, f32[3,3,256,256]{3,2,1,0:T(8,128)})) %all-reduce.5.cloned.1.call-update) | async-done | bytes 4718608 | tf_op jit(solution)/shard_map/psum | solution.py:139
  1043.5 5.1 broadcast_multiply_fusion
  (170 shorter events, 63.8 us)
Async XLA Ops:
  7.2 340.8 %copy-start = (bf16[3,3,256,256]{3,2,1,0:T(8,128)(2,1)S(1)}, bf16[3,3,256,256]{3,2,1,0:T(8,128)(2,1)}, u32[]{:S(2)}) copy-start(bf16[3,3,256,256]{3,2,1,0:T(8,128)(2,1)} %param.65) | copy-start | bytes 3538948
  9.6 12.8 %copy-start.10 = (bf16[16,64,256]{2,1,0:T(8,128)(2,1)S(1)}, bf16[16,64,256]{2,1,0:T(8,128)(2,1)}, u32[]{:S(2)}) copy-start(bf16[16,64,256]{2,1,0:T(8,128)(2,1)} %param.71) | copy-start | bytes 1572868
  9.6 12.8 %copy-start.22 = (s32[16,64]{1,0:T(8,128)S(1)}, s32[16,64]{1,0:T(8,128)}, u32[]{:S(2)}) copy-start(s32[16,64]{1,0:T(8,128)} %param.69) | copy-start | bytes 12292
  9.6 13.0 %copy-start.12 = (bf16[3,3,256,256]{3,2,1,0:T(8,128)(2,1)S(1)}, bf16[3,3,256,256]{3,2,1,0:T(8,128)(2,1)}, u32[]{:S(2)}) copy-start(bf16[3,3,256,256]{3,2,1,0:T(8,128)(2,1)} %param.67) | copy-start | bytes 3538948
  9.6 100.9 %all-to-all-start = ((bf16[64,64,256]{2,1,0:T(8,128)(2,1)}), bf16[64,64,256]{2,1,0:T(8,128)(2,1)}, u32[]{:S(2)}, u32[]{:S(2)}) async-start(bf16[64,64,256]{2,1,0:T(8,128)(2,1)} %stack.6), calls=%async_computation | async-start | bytes 4194304 | tf_op jit(solution)/shard_map/all_to_all | solution.py:35
  21.1 320.0 %all-gather.5.cloned.1.call-start = ((), (), s32[]{:S(2)}) async-start(), calls=%async_computation.2 | async-start | bytes 2129920 | tf_op jit(solution)/shard_map/all_gather | solution.py:43
  21.2 326.8 %copy-start.28 = (s32[256]{0:T(256)}, s32[256]{0:T(256)S(1)}, u32[]{:S(2)}) copy-start(s32[256]{0:T(256)S(1)} %and_select_fusion) | copy-start | bytes 3076
  24.1 3.6 copy-start.3
  80.1 3.6 collective-permute-start.8
  82.5 30.6 %copy-start.4 = (bf16[16,64,256]{2,1,0:T(8,128)(2,1)S(1)}, bf16[16,64,256]{2,1,0:T(8,128)(2,1)}, u32[]{:S(2)}) copy-start(bf16[16,64,256]{2,1,0:T(8,128)(2,1)} %param.64) | copy-start | bytes 1572868
  82.5 3.8 collective-permute-start.9
  92.3 23.7 %copy-start.16 = (bf16[1,64,256]{2,1,0:T(8,128)(2,1)S(1)}, bf16[1,64,256]{2,1,0:T(8,128)(2,1)}, u32[]{:S(2)}) copy-start(bf16[1,64,256]{2,1,0:T(8,128)(2,1)} %get-tuple-element.324) | copy-start | bytes 98308
  92.3 20.8 %collective-permute-start = (bf16[1,64,256]{2,1,0:T(8,128)(2,1)S(1)}, bf16[1,64,256]{2,1,0:T(8,128)(2,1)S(1)}, u32[]{:S(2)}, u32[]{:S(2)}) collective-permute-start(bf16[1,64,256]{2,1,0:T(8,128)(2,1)S(1)} %get-tuple-element.343), channel_id=1, source_target_pairs={{0,1},{1,2},{2,3},{4,5},{5,6},{6,7},{8,9},{9,10},{10,11},{12,13},{... | collective-permute-start | bytes 98312 | tf_op jit(solution)/shard_map/ppermute | solution.py:18
  99.4 13.7 %collective-permute-start.1 = (bf16[1,64,256]{2,1,0:T(8,128)(2,1)S(1)}, bf16[1,64,256]{2,1,0:T(8,128)(2,1)S(1)}, u32[]{:S(2)}, u32[]{:S(2)}) collective-permute-start(bf16[1,64,256]{2,1,0:T(8,128)(2,1)S(1)} %get-tuple-element.345), channel_id=1, source_target_pairs={{1,0},{2,1},{3,2},{5,4},{6,5},{7,6},{9,8},{10,9},{11,10},{13,12},{... | collective-permute-start | bytes 98312 | tf_op jit(solution)/shard_map/ppermute | solution.py:20
  102.1 245.8 %copy-start.25 = (pred[64]{0:T(512)(128)(4,1)}, pred[64]{0:T(512)(128)(4,1)S(1)}, u32[]{:S(2)}) copy-start(pred[64]{0:T(512)(128)(4,1)S(1)} %get-tuple-element.320) | copy-start | bytes 196
  102.1 243.0 %copy-start.27 = (s32[1024]{0:T(1024)}, s32[1024]{0:T(1024)S(1)}, u32[]{:S(2)}) copy-start(s32[1024]{0:T(1024)S(1)} %pad_clamp_fusion) | copy-start | bytes 12292
  102.1 13.9 %collective-permute-start.10 = (bf16[1,64,256]{2,1,0:T(8,128)(2,1)}, bf16[1,64,256]{2,1,0:T(8,128)(2,1)S(1)}, u32[]{:S(2)}, u32[]{:S(2)}) collective-permute-start(bf16[1,64,256]{2,1,0:T(8,128)(2,1)} %get-tuple-element.324), channel_id=1, source_target_pairs={{0,1},{1,2},{2,3},{4,5},{5,6},{6,7},{8,9},{9,10},{10,11},{12,13},{... | collective-permute-start | bytes 98312 | tf_op jit(solution)/shard_map/ppermute | solution.py:18
  108.6 7.4 collective-permute-start.11
  113.2 3.9 collective-permute-start.3
  113.3 3.8 collective-permute-start.2
  125.9 222.1 %copy-start.31 = (f32[256]{0:T(256)S(1)}, f32[256]{0:T(256)}, u32[]{:S(2)}) copy-start(f32[256]{0:T(256)} %param.66) | copy-start | bytes 3076
  355.4 12.8 %copy-start.14 = (bf16[16,64,256]{2,1,0:T(8,128)(2,1)S(1)}, bf16[16,64,256]{2,1,0:T(8,128)(2,1)}, u32[]{:S(2)}) copy-start(bf16[16,64,256]{2,1,0:T(8,128)(2,1)} %get-tuple-element.326) | copy-start | bytes 1572868
  355.4 124.9 %all-to-all-start.1 = ((bf16[64,64,256]{2,1,0:T(8,128)(2,1)}), bf16[64,64,256]{2,1,0:T(8,128)(2,1)}, u32[]{:S(2)}, u32[]{:S(2)}) async-start(bf16[64,64,256]{2,1,0:T(8,128)(2,1)} %stack.7), calls=%async_computation.1 | async-start | bytes 4194304 | tf_op jit(solution)/shard_map/all_to_all | solution.py:35
  368.1 345.1 %all-gather.7.cloned.1.call-start = ((), (), s32[]{:S(2)}) async-start(), calls=%async_computation.3 | async-start | bytes 2129920 | tf_op jit(solution)/shard_map/all_gather | solution.py:43
  369.6 3.6 copy-start.2
  405.0 6.3 copy-start.18
  405.0 6.3 copy-start.19
  405.0 3.4 collective-permute-start.12
  407.4 3.8 collective-permute-start.13
  408.3 2.9 copy-start.20
  414.4 61.4 %copy-start.6 = (f32[18,64,256]{2,1,0:T(8,128)}, f32[18,64,256]{2,1,0:T(8,128)S(1)}, u32[]{:S(2)}) copy-start(f32[18,64,256]{2,1,0:T(8,128)S(1)} %scatter-add.125) | copy-start | bytes 3538948
  415.1 628.4 %all-reduce.5.cloned.1.call-start = ((), (), s32[]{:S(2)}) async-start(), calls=%async_computation.4 | async-start | bytes 9437184 | tf_op jit(solution)/shard_map/psum | solution.py:139
  415.1 67.8 %collective-permute-start.5 = (bf16[1,64,256]{2,1,0:T(8,128)(2,1)}, bf16[1,64,256]{2,1,0:T(8,128)(2,1)S(1)}, u32[]{:S(2)}, u32[]{:S(2)}) collective-permute-start(bf16[1,64,256]{2,1,0:T(8,128)(2,1)} %get-tuple-element.342), channel_id=1, source_target_pairs={{1,0},{2,1},{3,2},{5,4},{6,5},{7,6},{9,8},{10,9},{11,10},{13,12},{... | collective-permute-start | bytes 98312 | tf_op jit(solution)/shard_map/ppermute | solution.py:20
  469.0 6.8 copy-start.24
  469.0 13.9 %copy-start.26 = (pred[64]{0:T(512)(128)(4,1)S(1)}, pred[64]{0:T(512)(128)(4,1)}, u32[]{:S(2)}) copy-start(pred[64]{0:T(512)(128)(4,1)} %copy-done.25) | copy-start | bytes 196
  469.0 17.0 %copy-start.15 = (bf16[16,64,256]{2,1,0:T(8,128)(2,1)S(1)}, bf16[16,64,256]{2,1,0:T(8,128)(2,1)}, u32[]{:S(2)}) copy-start(bf16[16,64,256]{2,1,0:T(8,128)(2,1)} %get-tuple-element.326) | copy-start | bytes 1572868
  475.8 7.2 collective-permute-start.4
  483.1 8.1 collective-permute-start.7
  483.4 7.8 collective-permute-start.6
  494.6 6.8 copy-start.9
  506.5 7.3 copy-start.7
  506.5 7.3 collective-permute-start.15
  508.6 6.2 collective-permute-start.14
  514.8 205.3 %copy-start.11 = (bf16[16,64,256]{2,1,0:T(8,128)(2,1)S(1)}, bf16[16,64,256]{2,1,0:T(8,128)(2,1)}, u32[]{:S(2)}) copy-start(bf16[16,64,256]{2,1,0:T(8,128)(2,1)} %param.71) | copy-start | bytes 1572868
  514.8 205.3 %copy-start.23 = (s32[16,64]{1,0:T(8,128)S(1)}, s32[16,64]{1,0:T(8,128)}, u32[]{:S(2)}) copy-start(s32[16,64]{1,0:T(8,128)} %param.69) | copy-start | bytes 12292
  514.8 205.3 %copy-start.29 = (s32[256]{0:T(256)S(1)}, s32[256]{0:T(256)}, u32[]{:S(2)}) copy-start(s32[256]{0:T(256)} %copy-done.28) | copy-start | bytes 3076
  717.0 4.2 copy-start.32
  1043.5 5.1 copy-start.1
  (6 other events, 9.1 us)
Sparse Core Ops, SparseCore 0:
  92.4 248.6 all-gather.4
  415.2 297.9 all-gather.6
  719.3 324.1 all-reduce.4
